TPU v7x, 256 devices: a whole 4x4x8 slice. The times are simulated.
256 devices in a mesh: dp: 4 (over y_lo, core), tm: 4 (over x), rows: 16 (over z, y_hi).
Axes of the slice: x: 4, y: 4 (y_hi: 2, y_lo: 2; y = y_hi * 2 + y_lo), z: 8, core: 2. Of those that a mesh axis runs over, the one named last changes fastest.
Arguments:
- latents: bfloat16 [4, 8, 16, 30, 512], P('dp', 'tm', 'rows'), may hold values from -6 to 6
- grad_out: bfloat16 [4, 8, 32, 60, 256], P('dp', 'tm', 'rows'), may hold values from -6 to 6
- kernel: bfloat16 [3, 3, 3, 512, 256], replicated, may hold values from -0.0546875 to 0.0546875
Outputs:
- grad_latents: bfloat16 [4, 8, 16, 30, 512], P('dp', 'tm', 'rows')
- weight_grad: float32 [512, 3, 3, 3, 256], P(('dp', 'tm', 'rows'))
All inputs are finite; a program needn't handle non-finite values.
Results may differ from a plain program's by a relative error of at most 0.001.
Values may be sent and summed in bfloat16 or wider, within the bound.
A program may use at most 128 MiB of HBM per device.

v0:
```python
import jax
import jax.numpy as jnp
from jax import lax
from jax.sharding import PartitionSpec as P


def shift_from(shard, axis, by):
    peers = lax.axis_size(axis)
    pairs = [(i, i + by) for i in range(peers) if 0 <= i + by < peers]
    return lax.ppermute(shard, axis, pairs)


def pool_pairs(values, dim):
    n = values.shape[dim] // 2
    pad = [(0, 0)] * values.ndim
    pad[dim] = (1, 1)
    ext = jnp.pad(values, pad)
    shape = values.shape
    shifted = ext.reshape(shape[:dim] + (n + 1, 2) + shape[dim + 1 :]).sum(axis=dim + 1)
    aligned = values.reshape(shape[:dim] + (n, 2) + shape[dim + 1 :]).sum(axis=dim + 1)
    out = [
        lax.slice_in_dim(shifted, 1, n + 1, axis=dim),
        aligned,
        lax.slice_in_dim(shifted, 0, n, axis=dim),
    ]
    return jnp.stack(out, axis=dim + 1)


def with_halo(block, axis, dim, width):
    count = lax.axis_size(axis)
    forward = [(i, i + 1) for i in range(count - 1)]
    backward = [(target, source) for source, target in forward]
    low = lax.ppermute(
        lax.slice_in_dim(block, block.shape[dim] - width, None, axis=dim), axis, forward
    )
    high = lax.ppermute(lax.slice_in_dim(block, 0, width, axis=dim), axis, backward)
    return jnp.concatenate([low, block, high], axis=dim)


def body(latents, grad_out, kernel):
    frames = grad_out.shape[1]
    height = grad_out.shape[2]
    width = grad_out.shape[3]
    channels = latents.shape[4]
    outputs = grad_out.shape[4]
    devices = lax.axis_size("dp") * lax.axis_size("tm") * lax.axis_size("rows")
    factor = float(devices * frames * height * width) ** (-0.5)
    slab_count = lax.axis_size("rows")
    grad_whole = lax.all_gather(grad_out[0], "rows", axis=1, tiled=True)
    whole_height = grad_whole.shape[1]
    near = with_halo(grad_out[0], "rows", 1, 1)
    later = shift_from(near, "tm", -1)
    grad_all = jnp.concatenate([near, later], axis=0)
    grad_all = jnp.pad(grad_all, ((0, 0), (0, 0), (1, 1), (0, 0)))
    patches = []
    for a in range(3):
        for i in range(3):
            for j in range(3):
                patches.append(
                    grad_all[2 - a : 2 - a + frames, 2 - i : 2 - i + height, 2 - j : 2 - j + width]
                )
    patches = jnp.stack(patches, axis=3).reshape(frames * height * width, 27, outputs)
    grad_up = lax.dot_general(
        patches,
        kernel.reshape(27, channels, outputs),
        (((1, 2), (0, 2)), ((), ())),
        preferred_element_type=jnp.float32,
    )
    pooled = grad_up.reshape(frames, height // 2, 2, width // 2, 2, channels).sum(axis=(2, 4))
    grad_latents = pooled.astype(jnp.bfloat16)[None]
    groups = lax.axis_size("dp") * lax.axis_size("tm")
    share = channels // devices
    earlier = shift_from(latents, "tm", 1)
    with_earlier = jnp.concatenate([earlier, latents], axis=1)
    lead = with_earlier.shape[:4]
    regrouped = with_earlier.reshape(lead + (groups, slab_count, share))
    regrouped = jnp.swapaxes(regrouped, 4, 5).reshape(lead + (channels,))
    owned = lax.all_to_all(regrouped, "rows", split_axis=4, concat_axis=2, tiled=True)[0]
    group_channels = owned.shape[3]
    taps_a = jnp.stack([owned[a : a + frames] for a in range(3)], axis=0)
    pooled_grad = pool_pairs(pool_pairs(grad_whole.astype(jnp.float32), 1), 3)
    scaled = pooled_grad * 65537.0
    top = scaled - (scaled - pooled_grad)
    both = jnp.stack([top, pooled_grad - top], axis=0).astype(jnp.bfloat16)
    term = jnp.einsum("afrsc,xfrisjo->caijxo", taps_a, both, preferred_element_type=jnp.float32)
    term = (term[..., 0, :] + term[..., 1, :]) * factor
    term = term.reshape(group_channels, 3, 3, 3, outputs)
    term = lax.psum_scatter(term, "dp", scatter_dimension=0, tiled=True)
    weight_grad = lax.psum_scatter(term, "tm", scatter_dimension=0, tiled=True)
    return (grad_latents, weight_grad)


def solution(mesh):
    in_specs = (P("dp", "tm", "rows", None, None), P("dp", "tm", "rows", None, None), P())
    out_specs = (P("dp", "tm", "rows", None, None), P(("dp", "tm", "rows"), None, None, None, None))
    return jax.shard_map(body, mesh=mesh, in_specs=in_specs, out_specs=out_specs, check_vma=False)
```

profile of v0, /device:TPU:8, one launch (start us, length us, event | category | flops | bytes accessed | tf_op | source)
XLA Modules:
  0.0 247.5 jit_solution(9366353959574920145)
XLA Ops:
  7.2 3.4 %collective-permute-start.3 = (bf16[1,2,1,30,512]{4,1,3,2,0:T(2,128)(2,1)}, bf16[1,2,1,30,512]{4,1,3,2,0:T(2,128)(2,1)S(1)}, u32[]{:S(2)}, u32[]{:S(2)}) collective-permute-start(bf16[1,2,1,30,512]{4,1,3,2,0:T(2,128)(2,1)} %param.3), channel_id=1, source_target_pairs={{0,16},{16,32},{32,48},{1,17},{17,33},{33,49},{2,18},{18,34},{34,5... | collective-permute-start | bytes 184328 | tf_op jit(solution)/shard_map/ppermute | solution.py:10
  10.6 1.2 fusion.25
  11.8 4.2 %collective-permute-start = (bf16[2,1,60,256]{3,1,2,0:T(2,128)(2,1)S(1)}, bf16[2,1,60,256]{3,1,2,0:T(2,128)(2,1)S(1)}, u32[]{:S(2)}, u32[]{:S(2)}) collective-permute-start(bf16[2,1,60,256]{3,1,2,0:T(2,128)(2,1)S(1)} %get-tuple-element.46), channel_id=1, source_target_pairs={{0,1},{1,2},{2,3},{3,4},{4,5},{5,6},{6,7},{7,8},{8,9},{9,10},{10,1... | collective-permute-start | bytes 184328 | tf_op jit(solution)/shard_map/ppermute | solution.py:33
  16.0 1.3 collective-permute-start.1
  17.3 1.6 copy.102
  19.0 1.3 dynamic-slice
  20.9 1.0 pad_maximum_fusion.5
  23.0 1.6 reshape.353
  24.7 12.5 %all-to-all-start = ((bf16[16,2,1920]{2,1,0:T(2,128)(2,1)}), bf16[16,2,1920]{2,1,0:T(2,128)(2,1)S(1)}, u32[]{:S(2)}, u32[]{:S(2)}) async-start(bf16[16,2,1920]{2,1,0:T(2,128)(2,1)} %reshape.353), calls=%async_computation | async-start | bytes 245760 | tf_op jit(solution)/shard_map/all_to_all | solution.py:78
  37.7 1.7 collective-permute-start.2
  39.9 8.4 %all-to-all-done = bf16[16,2,1920]{2,1,0:T(2,128)(2,1)S(1)} async-done(((bf16[16,2,1920]{2,1,0:T(2,128)(2,1)}), bf16[16,2,1920]{2,1,0:T(2,128)(2,1)S(1)}, u32[]{:S(2)}, u32[]{:S(2)}) %all-to-all-start) | async-done | bytes 122912 | tf_op jit(solution)/shard_map/all_to_all | solution.py:78
  48.4 1.4 reshape.354
  49.8 0.9 slice_bitcast_fusion.2
  51.4 0.7 pad_slice_fusion
  52.1 0.7 copy_dynamic-update-slice_fusion.26
  54.4 0.7 copy_dynamic-update-slice_fusion.23
  55.8 0.7 copy_dynamic-update-slice_fusion.21
  59.2 1.6 pad_slice_fusion.1
  61.5 0.7 copy_dynamic-update-slice_fusion.15
  62.8 0.7 copy_dynamic-update-slice_fusion.13
  64.2 0.7 copy_dynamic-update-slice_fusion.11
  64.9 0.7 copy_dynamic-update-slice_fusion.10
  66.3 0.7 copy_dynamic-update-slice_fusion.8
  66.9 41.3 %all-gather.3.cloned.1.call-done = bf16[1,2,32,60,256]{4,1,3,0,2:T(2,128)(2,1)} async-done(((bf16[1,2,2,60,256]{4,1,3,0,2:T(2,128)(2,1)}), bf16[1,2,32,60,256]{4,1,3,0,2:T(2,128)(2,1)}) %all-gather.3.cloned.1.call-update) | async-done | bytes 1966096 | tf_op jit(solution)/shard_map/all_gather | solution.py:49
  108.2 2.9 %convert_bitcast_fusion = f32[2,32,60,256]{3,0,2,1:T(2,128)S(1)} fusion(bf16[1,2,32,60,256]{4,1,3,0,2:T(2,128)(2,1)} %all-gather.3.cloned.1.call-done), kind=kLoop, calls=%fused_computation.21 | loop fusion | flops 983040 | bytes 5898240 | tf_op jit(solution)/shard_map/convert_element_type | solution.py:81
  111.1 3.4 %pad.13 = f32[2,34,60,256]{3,0,2,1:T(2,128)} pad(f32[2,32,60,256]{3,0,2,1:T(2,128)S(1)} %convert_bitcast_fusion, f32[]{:T(128)} %constant.3.clone.1), padding=0_0x1_1x0_0x0_0 | pad | bytes 8110084 | tf_op jit(solution)/shard_map/jit(_pad)/pad | solution.py:17
  114.5 5.3 %reduce_sum.46 = f32[2,17,60,256]{3,0,2,1:T(2,128)S(1)} reduce(f32[2,17,2,60,256]{4,0,3,2,1:T(2,128)} %bitcast.115, f32[]{:T(128)} %constant.3.clone.1), dimensions={2}, to_apply=%region_1.2 | reduce | flops 522240 | bytes 6266884 | tf_op jit(solution)/shard_map/reduce_sum | solution.py:19
  119.8 16.3 %fusion.23 = (f32[2,16,60,256]{3,0,2,1:T(2,128)}, f32[2,16,1,60,256]{4,0,3,1,2:T(2,128)}, f32[2,16,1,60,256]{4,0,3,1,2:T(2,128)}, f32[2,16,60,256]{3,0,2,1:T(2,128)}) fusion(f32[2,17,60,256]{3,0,2,1:T(2,128)S(1)} %reduce_sum.46), kind=kLoop, calls=%fused_computation.89 | loop fusion | bytes 11796480 | tf_op jit(solution)/shard_map/slice | solution.py:22
  136.1 4.7 %reduce_sum.47 = f32[2,16,60,256]{3,0,2,1:T(2,128)S(1)} reduce(bf16[2,16,2,60,256]{4,0,3,2,1:T(2,128)(2,1)} %bitcast.117, f32[]{:T(128)} %constant.3.clone.1), dimensions={2}, to_apply=%region_2.3 | reduce | flops 491520 | bytes 3932164 | tf_op jit(solution)/shard_map/reduce_sum | solution.py:20
  140.9 1.9 copy.106
  142.7 1.0 copy-done.4
  143.7 5.5 %select_maximum_fusion = f32[2,16,3,62,256]{4,0,3,1,2:T(2,128)} fusion(f32[2,16,1,60,256]{4,0,3,1,2:T(2,128)S(1)} %copy-done.4, f32[2,16,1,60,256]{4,0,3,1,2:T(2,128)S(1)} %bitcast.114, f32[2,16,1,60,256]{4,0,3,1,2:T(2,128)S(1)} %copy-done.3), kind=kLoop, calls=%fused_computation.10 | loop fusion | flops 12189696 | bytes 11993088 | tf_op jit(solution)/shard_map/stack | solution.py:26
  149.2 7.7 %reduce.2 = f32[2,16,3,31,256]{4,0,3,1,2:T(2,128)S(1)} reduce(f32[2,16,3,31,2,256]{5,0,4,3,1,2:T(2,128)} %bitcast.113, f32[]{:T(128)} %constant.3.clone.1), dimensions={4}, to_apply=%region_3.4 | reduce | flops 761856 | bytes 9142276
  156.9 1.5 fusion.22
  159.1 0.9 copy-done
  160.7 0.9 maximum_reduce_fusion
  161.5 1.7 copy.159
  163.2 1.0 copy_bitcast_fusion
  164.2 2.2 fusion.1
  166.5 1.7 fusion.8
  168.3 1.1 fusion.16
  171.5 0.7 copy_dynamic-update-slice_fusion.4
  172.2 0.7 copy_dynamic-update-slice_fusion.3
  174.9 12.6 %reduce-scatter.3.cloned.1.call-done = f32[8,3,3,3,256]{4,0,1,3,2:T(8,128)} async-done(((f32[32,3,3,3,256]{4,0,1,3,2:T(8,128)}), f32[8,3,3,3,256]{4,0,1,3,2:T(8,128)}) %reduce-scatter.3.cloned.1.call-update) | async-done | bytes 221200 | tf_op jit(solution)/shard_map/reduce_scatter | solution.py:88
  187.6 6.1 %fusion.12 = bf16[2,30,512]{2,1,0:T(8,128)(2,1)S(1)} fusion(bf16[27,512,256,1,1,1]{2,1,0,5,4,3:T(8,128)(2,1)} %bitcast.158, bf16[2,1,2,30,2,27,256]{6,3,5,4,2,0,1:T(8,128)(2,1)} %copy_dynamic-update-slice_fusion), kind=kOutput, calls=%fused_computation.20 | convolution fusion | flops 1698785280 | bytes 10457088 | tf_op jit(solution)/shard_map/dot_general | solution.py:63
  193.7 0.7 copy.114
  194.4 44.7 %all-reduce.6.cloned.1.call-done = f32[8,3,3,3,256]{4,0,1,3,2:T(8,128)} async-done(((f32[8,3,3,3,256]{4,0,1,3,2:T(8,128)}), f32[8,3,3,3,256]{4,0,1,3,2:T(8,128)}) %all-reduce.6.cloned.1.call-update) | async-done | bytes 221200
  239.1 1.0 constant_dynamic-slice_fusion
  (63 shorter events, 16.6 us)
Async XLA Ops:
  7.2 30.1 %copy-start.5 = (bf16[1,2,2,60,256]{4,2,3,1,0:T(2,128)(2,1)S(1)}, bf16[1,2,2,60,256]{4,2,3,1,0:T(2,128)(2,1)}, u32[]{:S(2)}) copy-start(bf16[1,2,2,60,256]{4,2,3,1,0:T(2,128)(2,1)} %param.4) | copy-start | bytes 368644
  7.2 101.0 %all-gather.3.cloned.1.call-start = ((), (), s32[]{:S(2)}) async-start(), calls=%async_computation.3 | async-start | bytes 2088960 | tf_op jit(solution)/shard_map/all_gather | solution.py:49
  7.2 13.7 %collective-permute-start.3 = (bf16[1,2,1,30,512]{4,1,3,2,0:T(2,128)(2,1)}, bf16[1,2,1,30,512]{4,1,3,2,0:T(2,128)(2,1)S(1)}, u32[]{:S(2)}, u32[]{:S(2)}) collective-permute-start(bf16[1,2,1,30,512]{4,1,3,2,0:T(2,128)(2,1)} %param.3), channel_id=1, source_target_pairs={{0,16},{16,32},{32,48},{1,17},{17,33},{33,49},{2,18},{18,34},{34,5... | collective-permute-start | bytes 184328 | tf_op jit(solution)/shard_map/ppermute | solution.py:10
  11.8 25.4 %collective-permute-start = (bf16[2,1,60,256]{3,1,2,0:T(2,128)(2,1)S(1)}, bf16[2,1,60,256]{3,1,2,0:T(2,128)(2,1)S(1)}, u32[]{:S(2)}, u32[]{:S(2)}) collective-permute-start(bf16[2,1,60,256]{3,1,2,0:T(2,128)(2,1)S(1)} %get-tuple-element.46), channel_id=1, source_target_pairs={{0,1},{1,2},{2,3},{3,4},{4,5},{5,6},{6,7},{7,8},{8,9},{9,10},{10,1... | collective-permute-start | bytes 184328 | tf_op jit(solution)/shard_map/ppermute | solution.py:33
  16.0 21.2 %collective-permute-start.1 = (bf16[2,1,60,256]{3,1,2,0:T(2,128)(2,1)S(1)}, bf16[2,1,60,256]{3,1,2,0:T(2,128)(2,1)S(1)}, u32[]{:S(2)}, u32[]{:S(2)}) collective-permute-start(bf16[2,1,60,256]{3,1,2,0:T(2,128)(2,1)S(1)} %get-tuple-element.47), channel_id=1, source_target_pairs={{1,0},{2,1},{3,2},{4,3},{5,4},{6,5},{7,6},{8,7},{9,8},{10,9},{11,1... | collective-permute-start | bytes 184328 | tf_op jit(solution)/shard_map/ppermute | solution.py:36
  24.7 23.7 %all-to-all-start = ((bf16[16,2,1920]{2,1,0:T(2,128)(2,1)}), bf16[16,2,1920]{2,1,0:T(2,128)(2,1)S(1)}, u32[]{:S(2)}, u32[]{:S(2)}) async-start(bf16[16,2,1920]{2,1,0:T(2,128)(2,1)} %reshape.353), calls=%async_computation | async-start | bytes 245760 | tf_op jit(solution)/shard_map/all_to_all | solution.py:78
  37.2 150.3 %reduce-scatter.3.cloned.1.call-start = ((), (), s32[]{:S(2)}) async-start(), calls=%async_computation.2 | async-start | bytes 1105920 | tf_op jit(solution)/shard_map/reduce_scatter | solution.py:88
  37.7 13.0 %collective-permute-start.2 = (bf16[2,4,60,256]{3,1,2,0:T(4,128)(2,1)S(1)}, bf16[2,4,60,256]{3,1,2,0:T(4,128)(2,1)S(1)}, u32[]{:S(2)}, u32[]{:S(2)}) collective-permute-start(bf16[2,4,60,256]{3,1,2,0:T(4,128)(2,1)S(1)} %pad_maximum_fusion.2), channel_id=1, source_target_pairs={{16,0},{32,16},{48,32},{17,1},{33,17},{49,33},{18,2},{34,18},{50,3... | collective-permute-start | bytes 737288 | tf_op jit(solution)/shard_map/ppermute | solution.py:10
  140.8 1.9 copy-start.3
  140.8 2.8 %copy-start.4 = (f32[2,16,1,60,256]{4,0,3,1,2:T(2,128)S(1)}, f32[2,16,1,60,256]{4,0,3,1,2:T(2,128)}, u32[]{:S(2)}) copy-start(f32[2,16,1,60,256]{4,0,3,1,2:T(2,128)} %get-tuple-element.16) | copy-start | bytes 5898244
  156.9 1.6 copy-start.1
  158.5 1.5 copy-start
  158.5 2.2 copy-start.2
  164.2 2.3 copy-start.10
  164.2 2.3 copy-start.11
  164.2 2.3 copy-start.12
  168.2 1.9 copy-start.9
  168.2 2.5 %copy-start.8 = (bf16[2,2,60,256]{3,1,2,0:T(2,128)(2,1)S(1)}, bf16[2,2,60,256]{3,1,2,0:T(2,128)(2,1)}, u32[]{:S(2)}) copy-start(bf16[2,2,60,256]{3,1,2,0:T(2,128)(2,1)} %get-tuple-element.37) | copy-start | bytes 368644
  168.2 3.9 %copy-start.7 = (bf16[2,2,60,256]{3,1,2,0:T(2,128)(2,1)S(1)}, bf16[2,2,60,256]{3,1,2,0:T(2,128)(2,1)}, u32[]{:S(2)}) copy-start(bf16[2,2,60,256]{3,1,2,0:T(2,128)(2,1)} %get-tuple-element.38) | copy-start | bytes 368644
  168.3 4.6 %copy-start.6 = (bf16[2,2,60,256]{3,1,2,0:T(2,128)(2,1)S(1)}, bf16[2,2,60,256]{3,1,2,0:T(2,128)(2,1)}, u32[]{:S(2)}) copy-start(bf16[2,2,60,256]{3,1,2,0:T(2,128)(2,1)} %get-tuple-element.31) | copy-start | bytes 368644
  169.4 69.7 %all-reduce.6.cloned.1.call-start = ((), (), s32[]{:S(2)}) async-start(), calls=%async_computation.4 | async-start | bytes 442368
Sparse Core Ops, SparseCore 0:
  19.1 89.0 all-gather.2
  169.5 17.9 reduce-scatter.2
  189.9 49.1 all-reduce.5
where the time goes:
time: 251 us; the launch traced here: 247 us
  waiting for transfers between devices  107 us (43%)
  local copies, waits for them, and re-layouts  61.5 us (25%)
  other arithmetic  32.8 us (13%)
  starting transfers between devices  23.2 us (9%)
  between operations  15 us (6%)
  matrix products  7.87 us (3%)
    unnamed x4, waiting for transfers between devices  44.8 us
    all_gather x1, waiting for transfers between devices, body(): grad_whole = lax.all_gather(grad_out[0], 'rows', axis=1, tiled=True)  41.3 us
    unnamed x59, local copies, waits for them, and re-layouts  27.8 us
    slice x3, local copies, waits for them, and re-layouts, pool_pairs(): lax.slice_in_dim(shifted, 1, n + 1, axis=dim)  18.5 us
    reduce_scatter x1, waiting for transfers between devices, body(): term = lax.psum_scatter(term, 'dp', scatter_dimension=0, tiled=True)  12.6 us
    all_to_all x1, starting transfers between devices, body(): lax.all_to_all(regrouped, 'rows', split_axis=4, concat_axis=2, tiled=True)  12.5 us
    all_to_all x1, waiting for transfers between devices, body(): lax.all_to_all(regrouped, 'rows', split_axis=4, concat_axis=2, tiled=True)  8.43 us
    unnamed x1, other arithmetic  7.74 us
  transfers between devices with their start and end apart: 8, of which 4 were waited for; matrix products, arithmetic and copies ran while one was open for 16% of the time, Pallas kernels for 0%

commit v1 on v0

--- a/solution.py
+++ b/solution.py
@@ -75,7 +75,12 @@
     lead = with_earlier.shape[:4]
     regrouped = with_earlier.reshape(lead + (groups, slab_count, share))
     regrouped = jnp.swapaxes(regrouped, 4, 5).reshape(lead + (channels,))
-    owned = lax.all_to_all(regrouped, "rows", split_axis=4, concat_axis=2, tiled=True)[0]
+    owned = jnp.concatenate(
+        lax.all_to_all(
+            jnp.stack(jnp.split(regrouped, lax.axis_size("rows"), axis=4)), "rows", 0, 0
+        ),
+        axis=2,
+    )[0]
     group_channels = owned.shape[3]
     taps_a = jnp.stack([owned[a : a + frames] for a in range(3)], axis=0)
     pooled_grad = pool_pairs(pool_pairs(grad_whole.astype(jnp.float32), 1), 3)

time: 251 us -> 236 us (0.940); the launches traced: 247 us -> 236 us
  local copies, waits for them, and re-layouts: 61.5 us -> 48.7 us
    slice x3, local copies, waits for them, and re-layouts: 18.5 us -> 6.54 us  [pool_pairs(): lax.slice_in_dim(shifted, 1, n + 1, axis=dim)]
    unnamed x59 -> x74, local copies, waits for them, and re-layouts: 27.8 us -> 26.3 us
where the time goes in v1:
time: 236 us
  waiting for transfers between devices  108 us (46%)
  local copies, waits for them, and re-layouts  48.7 us (21%)
  other arithmetic  32.8 us (14%)
  starting transfers between devices  23.5 us (10%)
  between operations  14.8 us (6%)
  matrix products  7.87 us (3%)
    unnamed x4, waiting for transfers between devices  44.8 us
    all_gather x1, waiting for transfers between devices, body(): grad_whole = lax.all_gather(grad_out[0], 'rows', axis=1, tiled=True)  41.9 us
    unnamed x74, local copies, waits for them, and re-layouts  26.3 us
    reduce_scatter x1, waiting for transfers between devices, body(): term = lax.psum_scatter(term, 'dp', scatter_dimension=0, tiled=True)  12.7 us
    all_to_all x1, starting transfers between devices, body(): lax.all_to_all(jnp.stack(jnp.split(regrouped, lax.axis_size('rows'), axis...  11.2 us
    all_to_all x1, waiting for transfers between devices, body(): lax.all_to_all(jnp.stack(jnp.split(regrouped, lax.axis_size('rows'), axis...  8.63 us
    unnamed x1, other arithmetic  7.74 us
    slice x3, local copies, waits for them, and re-layouts, pool_pairs(): lax.slice_in_dim(shifted, 1, n + 1, axis=dim)  6.54 us
  transfers between devices with their start and end apart: 8, of which 4 were waited for; matrix products, arithmetic and copies ran while one was open for 16% of the time, Pallas kernels for 0%

profile of v1, /device:TPU:8, one launch (start us, length us, event | category | flops | bytes accessed | tf_op | source)
XLA Modules:
  0.0 235.7 jit_solution(4671794044894006566)
XLA Ops:
  7.2 3.4 %collective-permute-start.3 = (bf16[1,2,1,30,512]{4,1,3,2,0:T(2,128)(2,1)}, bf16[1,2,1,30,512]{4,1,3,2,0:T(2,128)(2,1)S(1)}, u32[]{:S(2)}, u32[]{:S(2)}) collective-permute-start(bf16[1,2,1,30,512]{4,1,3,2,0:T(2,128)(2,1)} %param.3), channel_id=1, source_target_pairs={{0,16},{16,32},{32,48},{1,17},{17,33},{33,49},{2,18},{18,34},{34,5... | collective-permute-start | bytes 184328 | tf_op jit(solution)/shard_map/ppermute | solution.py:10
  10.6 1.2 fusion.25
  11.8 1.3 collective-permute-start.1
  13.1 6.1 %collective-permute-start = (bf16[2,1,60,256]{3,1,2,0:T(2,128)(2,1)S(1)}, bf16[2,1,60,256]{3,1,2,0:T(2,128)(2,1)S(1)}, u32[]{:S(2)}, u32[]{:S(2)}) collective-permute-start(bf16[2,1,60,256]{3,1,2,0:T(2,128)(2,1)S(1)} %get-tuple-element.46), channel_id=1, source_target_pairs={{0,1},{1,2},{2,3},{3,4},{4,5},{5,6},{6,7},{7,8},{8,9},{9,10},{10,1... | collective-permute-start | bytes 184328 | tf_op jit(solution)/shard_map/ppermute | solution.py:33
  19.2 1.6 copy.138
  20.9 1.3 dynamic-slice
  22.8 1.0 pad_maximum_fusion.5
  25.2 1.2 reshape.356
  26.4 11.2 %all-to-all-start = ((bf16[16,2,1920]{2,1,0:T(2,128)(2,1)}), bf16[16,2,1920]{2,1,0:T(2,128)(2,1)S(1)}, u32[]{:S(2)}, u32[]{:S(2)}) async-start(bf16[16,2,1920]{2,1,0:T(2,128)(2,1)} %reshape.356), calls=%async_computation | async-start | bytes 245760 | tf_op jit(solution)/shard_map/all_to_all | solution.py:79
  38.1 1.5 collective-permute-start.2
  40.1 8.6 %all-to-all-done = bf16[16,2,1920]{2,1,0:T(2,128)(2,1)S(1)} async-done(((bf16[16,2,1920]{2,1,0:T(2,128)(2,1)}), bf16[16,2,1920]{2,1,0:T(2,128)(2,1)S(1)}, u32[]{:S(2)}, u32[]{:S(2)}) %all-to-all-start) | async-done | bytes 122912 | tf_op jit(solution)/shard_map/all_to_all | solution.py:79
  49.5 0.9 slice_bitcast_fusion.2
  51.2 0.7 pad_slice_fusion
  51.9 0.7 copy_dynamic-update-slice_fusion.26
  54.2 0.7 copy_dynamic-update-slice_fusion.23
  55.5 0.7 copy_dynamic-update-slice_fusion.21
  58.9 1.6 pad_slice_fusion.1
  60.5 0.7 copy_dynamic-update-slice_fusion.16
  61.2 0.7 copy_dynamic-update-slice_fusion.15
  62.6 0.7 copy_dynamic-update-slice_fusion.13
  63.9 0.7 copy_dynamic-update-slice_fusion.11
  64.6 0.7 copy_dynamic-update-slice_fusion.10
  66.0 0.7 copy_dynamic-update-slice_fusion.8
  66.7 41.9 %all-gather.3.cloned.1.call-done = bf16[1,2,32,60,256]{4,1,3,0,2:T(2,128)(2,1)} async-done(((bf16[1,2,2,60,256]{4,1,3,0,2:T(2,128)(2,1)}), bf16[1,2,32,60,256]{4,1,3,0,2:T(2,128)(2,1)}) %all-gather.3.cloned.1.call-update) | async-done | bytes 1966096 | tf_op jit(solution)/shard_map/all_gather | solution.py:49
  108.6 2.9 %convert_bitcast_fusion = f32[2,32,60,256]{3,0,2,1:T(2,128)S(1)} fusion(bf16[1,2,32,60,256]{4,1,3,0,2:T(2,128)(2,1)} %all-gather.3.cloned.1.call-done), kind=kLoop, calls=%fused_computation.21 | loop fusion | flops 983040 | bytes 5898240 | tf_op jit(solution)/shard_map/convert_element_type | solution.py:86
  111.5 3.4 %pad.13 = f32[2,34,60,256]{3,0,2,1:T(2,128)} pad(f32[2,32,60,256]{3,0,2,1:T(2,128)S(1)} %convert_bitcast_fusion, f32[]{:T(128)} %constant.3.clone.1), padding=0_0x1_1x0_0x0_0 | pad | bytes 8110084 | tf_op jit(solution)/shard_map/jit(_pad)/pad | solution.py:17
  114.8 5.3 %reduce_sum.46 = f32[2,17,60,256]{3,0,2,1:T(2,128)S(1)} reduce(f32[2,17,2,60,256]{4,0,3,2,1:T(2,128)} %bitcast.175, f32[]{:T(128)} %constant.3.clone.1), dimensions={2}, to_apply=%region_1.2 | reduce | flops 522240 | bytes 6266884 | tf_op jit(solution)/shard_map/reduce_sum | solution.py:19
  120.2 4.4 %fusion.23 = (f32[2,16,60,256]{3,0,2,1:T(2,128)}, f32[2,16,1,60,256]{4,0,3,1,2:T(2,128)}, f32[2,16,1,60,256]{4,0,3,1,2:T(2,128)}, f32[2,16,60,256]{3,0,2,1:T(2,128)}) fusion(f32[2,17,60,256]{3,0,2,1:T(2,128)S(1)} %reduce_sum.46), kind=kLoop, calls=%fused_computation.121 | loop fusion | bytes 11796480 | tf_op jit(solution)/shard_map/slice | solution.py:22
  124.5 4.7 %reduce_sum.47 = f32[2,16,60,256]{3,0,2,1:T(2,128)S(1)} reduce(bf16[2,16,2,60,256]{4,0,3,2,1:T(2,128)(2,1)} %bitcast.177, f32[]{:T(128)} %constant.3.clone.1), dimensions={2}, to_apply=%region_2.3 | reduce | flops 491520 | bytes 3932164 | tf_op jit(solution)/shard_map/reduce_sum | solution.py:20
  129.3 1.9 copy.142
  131.2 1.0 copy-done.4
  132.1 5.5 %select_maximum_fusion = f32[2,16,3,62,256]{4,0,3,1,2:T(2,128)} fusion(f32[2,16,1,60,256]{4,0,3,1,2:T(2,128)S(1)} %copy-done.4, f32[2,16,1,60,256]{4,0,3,1,2:T(2,128)S(1)} %bitcast.174, f32[2,16,1,60,256]{4,0,3,1,2:T(2,128)S(1)} %copy-done.3), kind=kLoop, calls=%fused_computation.10 | loop fusion | flops 12189696 | bytes 11993088 | tf_op jit(solution)/shard_map/stack | solution.py:26
  137.6 7.7 %reduce.2 = f32[2,16,3,31,256]{4,0,3,1,2:T(2,128)S(1)} reduce(f32[2,16,3,31,2,256]{5,0,4,3,1,2:T(2,128)} %bitcast.173, f32[]{:T(128)} %constant.3.clone.1), dimensions={4}, to_apply=%region_3.4 | reduce | flops 761856 | bytes 9142276
  145.3 1.5 fusion.22
  147.6 0.9 copy-done
  149.1 0.9 maximum_reduce_fusion
  150.0 1.7 copy.194
  151.7 1.0 copy_bitcast_fusion
  152.6 2.3 fusion.1
  155.0 1.8 fusion.8
  156.8 1.1 fusion.16
  160.0 0.7 copy_dynamic-update-slice_fusion.4
  160.7 0.7 copy_dynamic-update-slice_fusion.3
  163.4 12.7 %reduce-scatter.3.cloned.1.call-done = f32[8,3,3,3,256]{4,0,1,3,2:T(8,128)} async-done(((f32[32,3,3,3,256]{4,0,1,3,2:T(8,128)}), f32[8,3,3,3,256]{4,0,1,3,2:T(8,128)}) %reduce-scatter.3.cloned.1.call-update) | async-done | bytes 221200 | tf_op jit(solution)/shard_map/reduce_scatter | solution.py:93
  176.1 6.1 %fusion.12 = bf16[2,30,512]{2,1,0:T(8,128)(2,1)S(1)} fusion(bf16[27,512,256,1,1,1]{2,1,0,5,4,3:T(8,128)(2,1)} %bitcast.233, bf16[2,1,2,30,2,27,256]{6,3,5,4,2,0,1:T(8,128)(2,1)} %copy_dynamic-update-slice_fusion), kind=kOutput, calls=%fused_computation.20 | convolution fusion | flops 1698785280 | bytes 10457088 | tf_op jit(solution)/shard_map/dot_general | solution.py:63
  182.2 0.7 copy.150
  182.9 44.7 %all-reduce.6.cloned.1.call-done = f32[8,3,3,3,256]{4,0,1,3,2:T(8,128)} async-done(((f32[8,3,3,3,256]{4,0,1,3,2:T(8,128)}), f32[8,3,3,3,256]{4,0,1,3,2:T(8,128)}) %all-reduce.6.cloned.1.call-update) | async-done | bytes 221200
  227.6 1.0 constant_dynamic-slice_fusion
  (79 shorter events, 16.9 us)
Async XLA Ops:
  7.2 30.5 %copy-start.5 = (bf16[1,2,2,60,256]{4,2,3,1,0:T(2,128)(2,1)S(1)}, bf16[1,2,2,60,256]{4,2,3,1,0:T(2,128)(2,1)}, u32[]{:S(2)}) copy-start(bf16[1,2,2,60,256]{4,2,3,1,0:T(2,128)(2,1)} %param.4) | copy-start | bytes 368644
  7.2 101.4 %all-gather.3.cloned.1.call-start = ((), (), s32[]{:S(2)}) async-start(), calls=%async_computation.3 | async-start | bytes 2088960 | tf_op jit(solution)/shard_map/all_gather | solution.py:49
  7.2 15.6 %collective-permute-start.3 = (bf16[1,2,1,30,512]{4,1,3,2,0:T(2,128)(2,1)}, bf16[1,2,1,30,512]{4,1,3,2,0:T(2,128)(2,1)S(1)}, u32[]{:S(2)}, u32[]{:S(2)}) collective-permute-start(bf16[1,2,1,30,512]{4,1,3,2,0:T(2,128)(2,1)} %param.3), channel_id=1, source_target_pairs={{0,16},{16,32},{32,48},{1,17},{17,33},{33,49},{2,18},{18,34},{34,5... | collective-permute-start | bytes 184328 | tf_op jit(solution)/shard_map/ppermute | solution.py:10
  11.8 25.8 %collective-permute-start.1 = (bf16[2,1,60,256]{3,1,2,0:T(2,128)(2,1)S(1)}, bf16[2,1,60,256]{3,1,2,0:T(2,128)(2,1)S(1)}, u32[]{:S(2)}, u32[]{:S(2)}) collective-permute-start(bf16[2,1,60,256]{3,1,2,0:T(2,128)(2,1)S(1)} %get-tuple-element.47), channel_id=1, source_target_pairs={{1,0},{2,1},{3,2},{4,3},{5,4},{6,5},{7,6},{8,7},{9,8},{10,9},{11,1... | collective-permute-start | bytes 184328 | tf_op jit(solution)/shard_map/ppermute | solution.py:36
  13.1 24.5 %collective-permute-start = (bf16[2,1,60,256]{3,1,2,0:T(2,128)(2,1)S(1)}, bf16[2,1,60,256]{3,1,2,0:T(2,128)(2,1)S(1)}, u32[]{:S(2)}, u32[]{:S(2)}) collective-permute-start(bf16[2,1,60,256]{3,1,2,0:T(2,128)(2,1)S(1)} %get-tuple-element.46), channel_id=1, source_target_pairs={{0,1},{1,2},{2,3},{3,4},{4,5},{5,6},{6,7},{7,8},{8,9},{9,10},{10,1... | collective-permute-start | bytes 184328 | tf_op jit(solution)/shard_map/ppermute | solution.py:33
  26.4 22.4 %all-to-all-start = ((bf16[16,2,1920]{2,1,0:T(2,128)(2,1)}), bf16[16,2,1920]{2,1,0:T(2,128)(2,1)S(1)}, u32[]{:S(2)}, u32[]{:S(2)}) async-start(bf16[16,2,1920]{2,1,0:T(2,128)(2,1)} %reshape.356), calls=%async_computation | async-start | bytes 245760 | tf_op jit(solution)/shard_map/all_to_all | solution.py:79
  37.6 138.5 %reduce-scatter.3.cloned.1.call-start = ((), (), s32[]{:S(2)}) async-start(), calls=%async_computation.2 | async-start | bytes 1105920 | tf_op jit(solution)/shard_map/reduce_scatter | solution.py:93
  38.1 12.4 %collective-permute-start.2 = (bf16[2,4,60,256]{3,1,2,0:T(4,128)(2,1)S(1)}, bf16[2,4,60,256]{3,1,2,0:T(4,128)(2,1)S(1)}, u32[]{:S(2)}, u32[]{:S(2)}) collective-permute-start(bf16[2,4,60,256]{3,1,2,0:T(4,128)(2,1)S(1)} %pad_maximum_fusion.2), channel_id=1, source_target_pairs={{16,0},{32,16},{48,32},{17,1},{33,17},{49,33},{18,2},{34,18},{50,3... | collective-permute-start | bytes 737288 | tf_op jit(solution)/shard_map/ppermute | solution.py:10
  129.3 1.9 copy-start.3
  129.3 2.8 %copy-start.4 = (f32[2,16,1,60,256]{4,0,3,1,2:T(2,128)S(1)}, f32[2,16,1,60,256]{4,0,3,1,2:T(2,128)}, u32[]{:S(2)}) copy-start(f32[2,16,1,60,256]{4,0,3,1,2:T(2,128)} %get-tuple-element.16) | copy-start | bytes 5898244
  145.3 1.6 copy-start.1
  146.9 1.5 copy-start
  146.9 2.2 copy-start.2
  152.6 2.3 copy-start.10
  152.6 2.3 copy-start.11
  152.6 2.3 copy-start.12
  156.7 1.9 copy-start.9
  156.8 2.5 %copy-start.8 = (bf16[2,2,60,256]{3,1,2,0:T(2,128)(2,1)S(1)}, bf16[2,2,60,256]{3,1,2,0:T(2,128)(2,1)}, u32[]{:S(2)}) copy-start(bf16[2,2,60,256]{3,1,2,0:T(2,128)(2,1)} %get-tuple-element.37) | copy-start | bytes 368644
  156.8 3.9 %copy-start.7 = (bf16[2,2,60,256]{3,1,2,0:T(2,128)(2,1)S(1)}, bf16[2,2,60,256]{3,1,2,0:T(2,128)(2,1)}, u32[]{:S(2)}) copy-start(bf16[2,2,60,256]{3,1,2,0:T(2,128)(2,1)} %get-tuple-element.38) | copy-start | bytes 368644
  156.8 4.6 %copy-start.6 = (bf16[2,2,60,256]{3,1,2,0:T(2,128)(2,1)S(1)}, bf16[2,2,60,256]{3,1,2,0:T(2,128)(2,1)}, u32[]{:S(2)}) copy-start(bf16[2,2,60,256]{3,1,2,0:T(2,128)(2,1)} %get-tuple-element.31) | copy-start | bytes 368644
  157.9 69.7 %all-reduce.6.cloned.1.call-start = ((), (), s32[]{:S(2)}) async-start(), calls=%async_computation.4 | async-start | bytes 442368
Sparse Core Ops, SparseCore 0:
  21.0 87.5 all-gather.2
  158.0 18.0 reduce-scatter.2
  178.4 49.1 all-reduce.5
